TPU v7x, 128 devices: a whole 4x4x4 slice. The times are simulated.
128 devices in a mesh: ctx: 16 (over y_hi, x, core), vocab: 8 (over y_lo, z).
Axes of the slice: x: 4, y: 4 (y_hi: 2, y_lo: 2; y = y_hi * 2 + y_lo), z: 4, core: 2. Of those that a mesh axis runs over, the one named last changes fastest.
Arguments:
- block_query: bfloat16 [512, 6144], P('ctx', 'vocab'), may hold values from -16 to 16
- block_key: bfloat16 [512, 6144], P('ctx', 'vocab'), may hold values from -16 to 16
- block_value: bfloat16 [512, 6144], P('ctx', 'vocab'), may hold values from -6 to 6
- block_doc: int32 [512], P('ctx'), may hold values from 0 to 1, never falling along the last dimension, each value on 1 to 480 neighbouring positions
- token_query: bfloat16 [2048, 6144], P(('ctx', 'vocab')), may hold values from -16 to 16
- token_key: bfloat16 [2048, 6144], P(('ctx', 'vocab')), may hold values from -16 to 16
- token_value: bfloat16 [2048, 6144], P(('ctx', 'vocab')), may hold values from -600 to 600
- token_state: bfloat16 [2048, 6144], P(('ctx', 'vocab')), may hold values from -6 to 6
- norm_gain: float32 [6144], replicated, may hold values from 0.5 to 1.5
- head_weight: bfloat16 [6144, 131072], P(None, ('ctx', 'vocab')), may hold values from -128 to 128
- targets: int32 [2048], replicated, may hold values from 0 to 131071
Outputs:
- block_context: bfloat16 [512, 6144], P('ctx', 'vocab')
- token_prior: float32 [2048], P(('ctx', 'vocab'))
Inputs may be any that keep to these rules, and one draw needn't show every extreme that they name: block_doc never falls along the blocks; no document holds more than 480 blocks.
All inputs are finite; a program needn't handle non-finite values.
Results may differ from a plain program's by a relative error of at most 0.005.
Values may be sent and summed in bfloat16 or wider, within the bound.
No kernel may reach another device: no remote copies, remote signals or barrier semaphores. Data moves between devices by JAX's collectives and lax.ppermute only.
A program may use at most 128 MiB of HBM per device.

v0:
```python
import math
import jax
import jax.numpy as jnp
from jax import lax
from jax.sharding import Mesh
from jax.sharding import PartitionSpec as P

HEAD_DIM = 128
BLOCK_LEN = 4
CTX = ("ctx_0", "ctx_1", "ctx_2")
VOCAB = ("vocab_0", "vocab_1")
CTX_VOCAB = ("ctx_0", "ctx_1", "ctx_2", "vocab_0", "vocab_1")
big_negative = -1e30


def sent_to_all(value, axis):
    size = lax.axis_size(axis)
    return lax.all_to_all(
        jnp.broadcast_to(value[None], (size, *value.shape)), axis, 0, 0, tiled=True
    )


def joined_along(pieces, dim):
    pieces = jnp.moveaxis(pieces, 0, dim)
    shape = pieces.shape
    return pieces.reshape(*shape[:dim], shape[dim] * shape[dim + 1], *shape[dim + 2 :])


def gathered_copies(value, axis, dim):
    pieces = sent_to_all(value, axis)
    return joined_along(pieces, dim)


def all_in_one(value, axis):
    leaves = jax.tree.leaves(value)
    sequence = sorted(range(len(leaves)), key=lambda k: -leaves[k].size)
    width = (1, *leaves[sequence[0]].shape)[-1]
    lines = [
        jnp.pad(leaves[k].reshape(-1), (0, -leaves[k].size % width)).reshape(-1, width)
        for k in sequence
    ]
    both, at, found = (lax.all_gather(jnp.concatenate(lines), axis), 0, {})
    for k, line in zip(sequence, lines):
        share = both[:, at : at + len(line)].reshape(len(both), -1)
        found[k] = share[:, : leaves[k].size].reshape(-1, *leaves[k].shape)
        at += len(line)
    numbers = iter(range(len(leaves)))
    return jax.tree.map(lambda _: found[next(numbers)], value)


def merged_by_axis(value, axes, combine):
    for axis in axes:
        pieces = all_in_one(value, axis)
        value = jax.tree.map(lambda part: part[0], pieces)
        for k in range(1, lax.axis_size(axis)):
            value = combine(value, jax.tree.map(lambda part: part[k], pieces))
    return value


def local_decoder(context, token_query, token_key, token_value, token_state, norm_gain):
    scale = 1.0 / math.sqrt(HEAD_DIM)
    groups = context.shape[0]
    width = context.shape[1]
    head_total = width // HEAD_DIM
    shape = (groups, BLOCK_LEN, head_total, HEAD_DIM)
    prefix = context.reshape(groups, 1, head_total, HEAD_DIM)
    queries = token_query.reshape(shape)
    keys = jnp.concatenate([prefix, token_key.reshape(shape)], axis=1)
    values = jnp.concatenate([prefix, token_value.reshape(shape)], axis=1)
    scores = (
        jnp.einsum("bihd,bjhd->bhij", queries, keys, preferred_element_type=jnp.float32) * scale
    )
    allowed = (
        jnp.arange(BLOCK_LEN + 1, dtype=jnp.int32)[None, :]
        <= jnp.arange(BLOCK_LEN, dtype=jnp.int32)[:, None] + 1
    )
    scores = jnp.where(allowed, scores, -jnp.inf)
    highest = jnp.max(scores, axis=-1, keepdims=True)
    weights = jnp.exp(scores - highest)
    totals = jnp.sum(weights, axis=-1)
    mixed = jnp.einsum(
        "bhij,bjhd->bihd", weights.astype(jnp.bfloat16), values, preferred_element_type=jnp.float32
    )
    mixed = mixed / jnp.transpose(totals, (0, 2, 1))[..., None]
    summed = token_state.astype(jnp.float32) + mixed.reshape(groups * BLOCK_LEN, width)
    power = jnp.mean(summed * summed, axis=-1, keepdims=True)
    return (summed * lax.rsqrt(power + 1e-05) * norm_gain).astype(jnp.bfloat16)


def local(
    block_query,
    block_key,
    block_value,
    block_doc,
    token_query,
    token_key,
    token_value,
    token_state,
    norm_gain,
    head_weight,
    targets,
):
    local_rows = block_query.shape[0]
    head_count = block_query.shape[1] // HEAD_DIM
    scale = 1.0 / math.sqrt(HEAD_DIM)
    first_row = lax.axis_index(CTX) * local_rows
    queries = block_query.reshape(local_rows, head_count, HEAD_DIM)
    own_doc = block_doc.astype(jnp.bfloat16)
    query_places = first_row + jnp.arange(local_rows, dtype=jnp.int32)
    highest = jnp.full((local_rows, head_count), big_negative, jnp.float32)
    keys = lax.all_gather(block_key, CTX, axis=0, tiled=True)
    values = lax.all_gather(block_value, CTX, axis=0, tiled=True)
    docs = lax.all_gather(own_doc, CTX, axis=0, tiled=True)
    count = keys.shape[0]
    keys = keys.reshape(count, head_count, HEAD_DIM)
    values = values.reshape(count, head_count, HEAD_DIM)
    scores = jnp.einsum("qhd,khd->qhk", queries, keys, preferred_element_type=jnp.float32) * scale
    key_places = jnp.arange(count, dtype=jnp.int32)
    allowed = (query_places[:, None] >= key_places[None, :]) & (own_doc[:, None] == docs[None, :])
    allowed = allowed[:, None, :]
    newest = jnp.maximum(highest, jnp.max(jnp.where(allowed, scores, big_negative), axis=-1))
    weights = jnp.where(allowed, jnp.exp(scores - newest[..., None]), 0.0)
    totals = jnp.sum(weights, axis=-1)
    update = jnp.einsum(
        "qhk,khd->qhd", weights.astype(jnp.bfloat16), values, preferred_element_type=jnp.float32
    )
    mixed = update
    highest, totals, mixed = (newest, totals, mixed)
    block_context = (
        (mixed / totals[..., None]).reshape(local_rows, head_count * HEAD_DIM).astype(jnp.bfloat16)
    )
    grouped = lax.all_to_all(block_context, VOCAB, split_axis=0, concat_axis=1, tiled=True)
    hidden = local_decoder(grouped, token_query, token_key, token_value, token_state, norm_gain)
    vocab_cols = head_weight.shape[1]
    col_start = lax.axis_index(CTX_VOCAB) * vocab_cols
    columns = jnp.arange(vocab_cols, dtype=jnp.int32)
    group_states = gathered_copies(hidden, VOCAB, 0)
    piece = lax.all_gather(group_states, CTX, axis=0, tiled=True)
    logits = jnp.dot(piece, head_weight, preferred_element_type=jnp.float32)
    top = jnp.max(logits, axis=-1)
    mass = jnp.sum(jnp.exp(logits - top[:, None]), axis=-1)
    wanted = targets - col_start
    picked = jnp.sum(jnp.where(columns[None, :] == wanted[:, None], logits, 0.0), axis=1)
    peaks = top
    masses = mass
    picks = picked
    stats = (peaks, masses, picks)

    def combine(left, right):
        top = jnp.maximum(left[0], right[0])
        mass = left[1] * jnp.exp(left[0] - top) + right[1] * jnp.exp(right[0] - top)
        return (top, mass, left[2] + right[2])

    peaks, masses, picks = merged_by_axis(stats, CTX_VOCAB, combine)
    priors = picks - (peaks + jnp.log(masses))
    own_count = hidden.shape[0]
    token_prior = lax.dynamic_slice_in_dim(priors, lax.axis_index(CTX_VOCAB) * own_count, own_count)
    return (block_context, token_prior)


def solution(mesh):
    torus = Mesh(
        mesh.devices.reshape(2, 4, 2, 2, 4), ("ctx_0", "ctx_1", "ctx_2", "vocab_0", "vocab_1")
    )
    in_specs = (
        P(CTX, VOCAB),
        P(CTX, VOCAB),
        P(CTX, VOCAB),
        P(CTX),
        P(CTX_VOCAB, None),
        P(CTX_VOCAB, None),
        P(CTX_VOCAB, None),
        P(CTX_VOCAB, None),
        P(),
        P(None, CTX_VOCAB),
        P(),
    )
    out_specs = (P(CTX, VOCAB), P(CTX_VOCAB))
    return jax.shard_map(local, mesh=torus, in_specs=in_specs, out_specs=out_specs, check_vma=False)
```

profile of v0, /device:TPU:0, one launch (start us, length us, event | category | flops | bytes accessed | tf_op | source)
XLA Modules:
  0.0 360.8 jit_solution(2283637337288649313)
XLA Ops:
  7.2 0.8 convert_element_type.25
  8.0 1.2 dynamic-slice
  10.1 38.1 %all-reduce = bf16[512]{0:T(512)(128)(2,1)S(1)} all-reduce(bf16[512]{0:T(512)(128)(2,1)S(1)} %dynamic-update-slice), channel_id=1, replica_groups=mesh['ctx_0'=2,'ctx_1'=4,'ctx_2'=2,'vocab_0'=2,'vocab_1'=4] {'ctx_0','ct..., use_global_device_ids=true, to_apply=%add | all-reduce | flops 512 | bytes 2048
  48.2 21.7 %all_gather.43 = bf16[512,768]{1,0:T(8,128)(2,1)S(1)} all-gather(bf16[32,768]{1,0:T(8,128)(2,1)} %param.12), channel_id=1, replica_groups=mesh['ctx_0'=2,'ctx_1'=4,'ctx_2'=2,'vocab_0'=2,'vocab_1'=4] {'ctx_0','ct..., dimensions={0}, use_global_device_ids=true | all-gather | bytes 835584 | tf_op jit(solution)/shard_map/all_gather | solution.py:111
  70.6 23.0 %all_gather.44 = bf16[512,768]{1,0:T(8,128)(2,1)S(1)} all-gather(bf16[32,768]{1,0:T(8,128)(2,1)} %param.13), channel_id=1, replica_groups=mesh['ctx_0'=2,'ctx_1'=4,'ctx_2'=2,'vocab_0'=2,'vocab_1'=4] {'ctx_0','ct..., dimensions={0}, use_global_device_ids=true | all-gather | bytes 835584 | tf_op jit(solution)/shard_map/all_gather | solution.py:112
  94.1 0.4 fusion.5
  94.6 0.7 convert_element_type.30
  95.2 5.4 %all-to-all-start = ((bf16[8,4,768]{2,1,0:T(4,128)(2,1)}), bf16[8,4,768]{2,1,0:T(4,128)(2,1)S(1)}, u32[]{:S(2)}, u32[]{:S(2)}) async-start(bf16[8,4,768]{2,1,0:T(4,128)(2,1)} %convert_element_type.30), calls=%async_computation | async-start | bytes 98304 | tf_op jit(solution)/shard_map/all_to_all | solution.py:132
  100.8 1.0 copy.48
  102.0 4.9 %all-to-all-done = bf16[8,4,768]{2,1,0:T(4,128)(2,1)S(1)} async-done(((bf16[8,4,768]{2,1,0:T(4,128)(2,1)}), bf16[8,4,768]{2,1,0:T(4,128)(2,1)S(1)}, u32[]{:S(2)}, u32[]{:S(2)}) %all-to-all-start) | async-done | bytes 49184 | tf_op jit(solution)/shard_map/all_to_all | solution.py:132
  107.0 0.5 fusion.61
  107.5 0.5 fusion.10
  108.0 0.6 fusion
  109.2 23.8 %all_to_all.18 = bf16[8,16,6144]{2,1,0:T(8,128)(2,1)} all-to-all(bf16[8,16,6144]{2,1,0:T(8,128)(2,1)S(1)} %broadcast_in_dim.61), channel_id=1, replica_groups=mesh['ctx_0'=2,'ctx_1'=4,'ctx_2'=2,'vocab_0'=2,'vocab_1'=4] {'vocab_0','..., dimensions={0} | all-to-all | bytes 3145728 | tf_op jit(solution)/shard_map/all_to_all | solution.py:18
  133.1 0.6 copy_bitcast_fusion
  133.7 143.4 %all-gather.12.cloned.1.call-done = bf16[2048,6144]{1,0:T(8,128)(2,1)} async-done(((bf16[128,6144]{1,0:T(8,128)(2,1)}), bf16[2048,6144]{1,0:T(8,128)(2,1)}) %all-gather.12.cloned.1.call-update) | async-done | bytes 25165840 | tf_op jit(solution)/shard_map/all_gather | solution.py:138
  277.1 34.1 %fusion.62 = (f32[2048]{0:T(1024)S(1)}, f32[2048,1024]{0,1:T(8,128)}) fusion(bf16[2048,6144]{1,0:T(8,128)(2,1)} %all-gather.12.cloned.1.call-done, bf16[6144,1024]{1,0:T(8,128)(2,1)} %param.20), kind=kOutput, calls=%fused_computation.121 | convolution fusion | flops 25771898880 | bytes 46145536 | tf_op jit(solution)/shard_map/dot_general | solution.py:139
  311.2 4.6 %exponential_reduce_fusion = (f32[2048]{0:T(1024)S(1)}, f32[2048]{0:T(1024)S(1)}) fusion(f32[2048,1024]{0,1:T(8,128)} %get-tuple-element.31, f32[2048]{0:T(1024)S(1)} %get-tuple-element.30, s32[2048]{0:T(1024)S(1)} %broadcast_subtract_fusion), kind=kLoop, calls=%fused_computation.2 | loop fusion | flops 10481664 | bytes 8421376 | tf_op jit(solution)/shard_map/reduce_sum | solution.py:141
  315.8 6.1 %all-gather.5 = f32[2,3,2048]{2,1,0:T(4,128)S(1)} all-gather(f32[1,3,2048]{2,1,0:T(4,128)S(1)} %maximum_bitcast_fusion), channel_id=2, replica_groups=mesh['ctx_0'=2,'ctx_1'=4,'ctx_2'=2,'vocab_0'=2,'vocab_1'=4] {'ctx_0'}, dimensions={0}, use_global_device_ids=true | all-gather | bytes 73728 | tf_op jit(solution)/shard_map/all_gather | solution.py:42
  322.0 12.0 %all-gather.6 = f32[4,3,2048]{2,1,0:T(4,128)S(1)} all-gather(f32[1,3,2048]{2,1,0:T(4,128)S(1)} %maximum_bitcast_fusion.1), channel_id=3, replica_groups=mesh['ctx_0'=2,'ctx_1'=4,'ctx_2'=2,'vocab_0'=2,'vocab_1'=4] {'ctx_1'}, dimensions={0}, use_global_device_ids=true | all-gather | bytes 122880 | tf_op jit(solution)/shard_map/all_gather | solution.py:42
  334.2 1.9 all-gather.7
  336.1 4.6 %all-gather.8 = f32[2,3,2048]{2,1,0:T(4,128)S(1)} all-gather(f32[1,3,2048]{2,1,0:T(4,128)S(1)} %maximum_bitcast_fusion.3), channel_id=5, replica_groups=mesh['ctx_0'=2,'ctx_1'=4,'ctx_2'=2,'vocab_0'=2,'vocab_1'=4] {'vocab_0'}, dimensions={0}, use_global_device_ids=true | all-gather | bytes 73728 | tf_op jit(solution)/shard_map/all_gather | solution.py:42
  340.8 12.5 %all-gather.9 = f32[4,3,2048]{2,1,0:T(4,128)S(1)} all-gather(f32[1,3,2048]{2,1,0:T(4,128)S(1)} %maximum_bitcast_fusion.4), channel_id=6, replica_groups=mesh['ctx_0'=2,'ctx_1'=4,'ctx_2'=2,'vocab_0'=2,'vocab_1'=4] {'vocab_1'}, dimensions={0}, use_global_device_ids=true | all-gather | bytes 122880 | tf_op jit(solution)/shard_map/all_gather | solution.py:42
  353.4 0.6 dynamic-slice_subtract_fusion
  (55 shorter events, 3.0 us)
Async XLA Ops:
  7.2 63.1 %copy-start = (bf16[32,768]{1,0:T(8,128)(2,1)S(1)}, bf16[32,768]{1,0:T(8,128)(2,1)}, u32[]{:S(2)}) copy-start(bf16[32,768]{1,0:T(8,128)(2,1)} %param.11) | copy-start | bytes 147460
  7.2 94.6 %copy-start.2 = (bf16[16,6144]{1,0:T(8,128)(2,1)S(1)}, bf16[16,6144]{1,0:T(8,128)(2,1)}, u32[]{:S(2)}) copy-start(bf16[16,6144]{1,0:T(8,128)(2,1)} %param.15) | copy-start | bytes 589828
  7.2 94.7 %copy-start.3 = (bf16[16,6144]{1,0:T(8,128)(2,1)S(1)}, bf16[16,6144]{1,0:T(8,128)(2,1)}, u32[]{:S(2)}) copy-start(bf16[16,6144]{1,0:T(8,128)(2,1)} %param.17) | copy-start | bytes 589828
  69.9 38.7 %copy-start.1 = (bf16[16,6144]{1,0:T(8,128)(2,1)S(1)}, bf16[16,6144]{1,0:T(8,128)(2,1)}, u32[]{:S(2)}) copy-start(bf16[16,6144]{1,0:T(8,128)(2,1)} %param.18) | copy-start | bytes 589828
  70.2 38.7 %copy-start.4 = (f32[6144]{0:T(1024)S(1)}, f32[6144]{0:T(1024)}, u32[]{:S(2)}) copy-start(f32[6144]{0:T(1024)} %param.19) | copy-start | bytes 73732
  95.2 11.7 %all-to-all-start = ((bf16[8,4,768]{2,1,0:T(4,128)(2,1)}), bf16[8,4,768]{2,1,0:T(4,128)(2,1)S(1)}, u32[]{:S(2)}, u32[]{:S(2)}) async-start(bf16[8,4,768]{2,1,0:T(4,128)(2,1)} %convert_element_type.30), calls=%async_computation | async-start | bytes 98304 | tf_op jit(solution)/shard_map/all_to_all | solution.py:132
  100.6 176.4 %all-gather.12.cloned.1.call-start = ((), (), s32[]{:S(2)}) async-start(), calls=%async_computation.2 | async-start | bytes 26738688 | tf_op jit(solution)/shard_map/all_gather | solution.py:138
  101.9 31.2 %copy-start.5 = (s32[2048]{0:T(1024)S(1)}, s32[2048]{0:T(1024)}, u32[]{:S(2)}) copy-start(s32[2048]{0:T(1024)} %param.21) | copy-start | bytes 24580
Sparse Core Ops, SparseCore 0:
  133.2 143.8 all-gather.11
where the time goes:
time: 361 us
  waiting for transfers between devices  148 us (41%)
  blocking collectives  144 us (40%)
  matrix products  35.9 us (10%)
  between operations  15.1 us (4%)
  other arithmetic  7.79 us (2%)
  starting transfers between devices  5.47 us (2%)
  local copies, waits for them, and re-layouts  4.76 us (1%)
    all_gather x1, waiting for transfers between devices, local(): piece = lax.all_gather(group_states, CTX, axis=0, tiled=True)  143 us
    unnamed x1, blocking collectives  38.1 us
    all_gather x5, blocking collectives, all_in_one(): both, at, found = (lax.all_gather(jnp.concatenate(lines), axis), 0, {})  37 us
    dot_general x1, matrix products, local(): logits = jnp.dot(piece, head_weight, preferred_element_type=jnp.float32)  34.1 us
    all_to_all x1, blocking collectives, sent_to_all(): lax.all_to_all(jnp.broadcast_to(value[None], (size, *value.shape)), axis,...  23.8 us
    all_gather x1, blocking collectives, local(): values = lax.all_gather(block_value, CTX, axis=0, tiled=True)  23 us
    all_gather x1, blocking collectives, local(): keys = lax.all_gather(block_key, CTX, axis=0, tiled=True)  21.7 us
  transfers between devices with their start and end apart: 2, of which 2 were waited for; matrix products, arithmetic and copies ran while one was open for 1% of the time, Pallas kernels for 0%

commit v1 on v0

--- a/solution.py
+++ b/solution.py
@@ -109,7 +109,10 @@
     query_places = first_row + jnp.arange(local_rows, dtype=jnp.int32)
     highest = jnp.full((local_rows, head_count), big_negative, jnp.float32)
     keys = lax.all_gather(block_key, CTX, axis=0, tiled=True)
-    values = lax.all_gather(block_value, CTX, axis=0, tiled=True)
+    peers = lax.axis_size(CTX)
+    tiles = jnp.stack([block_value for _ in range(peers)])
+    tiles = lax.all_to_all(tiles, CTX, split_axis=0, concat_axis=0)
+    values = jnp.concatenate(tiles, axis=0)
     docs = lax.all_gather(own_doc, CTX, axis=0, tiled=True)
     count = keys.shape[0]
     keys = keys.reshape(count, head_count, HEAD_DIM)

time: 361 us -> 350 us (0.970)
  blocking collectives: 144 us -> 121 us
  starting transfers between devices: 5.47 us -> 12.6 us
    all_gather x1 -> x0, blocking collectives: 23 us -> none  [local(): values = lax.all_gather(block_value, CTX, axis=0, tiled=True)]
    all_to_all x0 -> x1, starting transfers between devices: none -> 7.15 us  [local(): tiles = lax.all_to_all(tiles, CTX, split_axis=0, concat_axis=0)]
  transfers between devices with their start and end apart: 2 -> 3, of which waited for: 2 -> 2; matrix products, arithmetic and copies ran while one was open for 1% -> 1% of each run, Pallas kernels for 0% -> 0%
where the time goes in v1:
time: 350 us; the launch traced here: 349 us
  waiting for transfers between devices  151 us (43%)
  blocking collectives  121 us (35%)
  matrix products  35.8 us (10%)
  between operations  15.1 us (4%)
  starting transfers between devices  12.6 us (4%)
  other arithmetic  7.72 us (2%)
  local copies, waits for them, and re-layouts  6.26 us (2%)
    all_gather x1, waiting for transfers between devices, local(): piece = lax.all_gather(group_states, CTX, axis=0, tiled=True)  145 us
    unnamed x1, blocking collectives  38.4 us
    all_gather x5, blocking collectives, all_in_one(): both, at, found = (lax.all_gather(jnp.concatenate(lines), axis), 0, {})  37 us
    dot_general x1, matrix products, local(): logits = jnp.dot(piece, head_weight, preferred_element_type=jnp.float32)  34.1 us
    all_to_all x1, blocking collectives, sent_to_all(): lax.all_to_all(jnp.broadcast_to(value[None], (size, *value.shape)), axis,...  23.8 us
    all_gather x1, blocking collectives, local(): keys = lax.all_gather(block_key, CTX, axis=0, tiled=True)  21.7 us
    all_to_all x1, starting transfers between devices, local(): tiles = lax.all_to_all(tiles, CTX, split_axis=0, concat_axis=0)  7.15 us
  transfers between devices with their start and end apart: 3, of which 2 were waited for; matrix products, arithmetic and copies ran while one was open for 1% of the time, Pallas kernels for 0%

profile of v1, /device:TPU:0, one launch (start us, length us, event | category | flops | bytes accessed | tf_op | source)
XLA Modules:
  0.0 349.3 jit_solution(6851544545165855082)
XLA Ops:
  7.2 1.8 stack.2
  9.0 7.1 %all-to-all-start = ((bf16[16,32,768]{2,1,0:T(8,128)(2,1)}), bf16[16,32,768]{2,1,0:T(8,128)(2,1)S(1)}, u32[]{:S(2)}, u32[]{:S(2)}) async-start(bf16[16,32,768]{2,1,0:T(8,128)(2,1)} %stack.2), calls=%async_computation | async-start | bytes 1572864 | tf_op jit(solution)/shard_map/all_to_all | solution.py:114
  16.2 0.7 convert_element_type.25
  16.9 1.2 dynamic-slice
  19.0 38.4 %all-reduce = bf16[512]{0:T(512)(128)(2,1)S(1)} all-reduce(bf16[512]{0:T(512)(128)(2,1)S(1)} %dynamic-update-slice), channel_id=1, replica_groups=mesh['ctx_0'=2,'ctx_1'=4,'ctx_2'=2,'vocab_0'=2,'vocab_1'=4] {'ctx_0','ct..., use_global_device_ids=true, to_apply=%add | all-reduce | flops 512 | bytes 2048
  57.4 21.7 %all_gather.40 = bf16[512,768]{1,0:T(8,128)(2,1)S(1)} all-gather(bf16[32,768]{1,0:T(8,128)(2,1)} %param.12), channel_id=1, replica_groups=mesh['ctx_0'=2,'ctx_1'=4,'ctx_2'=2,'vocab_0'=2,'vocab_1'=4] {'ctx_0','ct..., dimensions={0}, use_global_device_ids=true | all-gather | bytes 835584 | tf_op jit(solution)/shard_map/all_gather | solution.py:111
  80.1 0.9 reshape_reshape.3
  81.3 0.7 convert_element_type.30
  82.0 5.4 %all-to-all-start.1 = ((bf16[8,4,768]{2,1,0:T(4,128)(2,1)}), bf16[8,4,768]{2,1,0:T(4,128)(2,1)S(1)}, u32[]{:S(2)}, u32[]{:S(2)}) async-start(bf16[8,4,768]{2,1,0:T(4,128)(2,1)} %convert_element_type.30), calls=%async_computation.1 | async-start | bytes 98304 | tf_op jit(solution)/shard_map/all_to_all | solution.py:135
  87.9 5.9 %all-to-all-done.1 = bf16[8,4,768]{2,1,0:T(4,128)(2,1)S(1)} async-done(((bf16[8,4,768]{2,1,0:T(4,128)(2,1)}), bf16[8,4,768]{2,1,0:T(4,128)(2,1)S(1)}, u32[]{:S(2)}, u32[]{:S(2)}) %all-to-all-start.1) | async-done | bytes 49184 | tf_op jit(solution)/shard_map/all_to_all | solution.py:135
  93.8 0.5 fusion.62
  94.3 0.5 fusion.11
  94.8 0.6 fusion
  96.0 23.8 %all_to_all.23 = bf16[8,16,6144]{2,1,0:T(8,128)(2,1)} all-to-all(bf16[8,16,6144]{2,1,0:T(8,128)(2,1)S(1)} %broadcast_in_dim.61), channel_id=1, replica_groups=mesh['ctx_0'=2,'ctx_1'=4,'ctx_2'=2,'vocab_0'=2,'vocab_1'=4] {'vocab_0','..., dimensions={0} | all-to-all | bytes 3145728 | tf_op jit(solution)/shard_map/all_to_all | solution.py:18
  119.9 0.6 copy_bitcast_fusion
  120.5 145.1 %all-gather.12.cloned.1.call-done = bf16[2048,6144]{1,0:T(8,128)(2,1)} async-done(((bf16[128,6144]{1,0:T(8,128)(2,1)}), bf16[2048,6144]{1,0:T(8,128)(2,1)}) %all-gather.12.cloned.1.call-update) | async-done | bytes 25165840 | tf_op jit(solution)/shard_map/all_gather | solution.py:141
  265.6 34.1 %fusion.63 = (f32[2048]{0:T(1024)S(1)}, f32[2048,1024]{0,1:T(8,128)}) fusion(bf16[2048,6144]{1,0:T(8,128)(2,1)} %all-gather.12.cloned.1.call-done, bf16[6144,1024]{1,0:T(8,128)(2,1)} %param.20), kind=kOutput, calls=%fused_computation.122 | convolution fusion | flops 25771898880 | bytes 46145536 | tf_op jit(solution)/shard_map/dot_general | solution.py:142
  299.7 4.6 %exponential_reduce_fusion = (f32[2048]{0:T(1024)S(1)}, f32[2048]{0:T(1024)S(1)}) fusion(f32[2048,1024]{0,1:T(8,128)} %get-tuple-element.31, f32[2048]{0:T(1024)S(1)} %get-tuple-element.30, s32[2048]{0:T(1024)S(1)} %broadcast_subtract_fusion), kind=kLoop, calls=%fused_computation.2 | loop fusion | flops 10481664 | bytes 8421376 | tf_op jit(solution)/shard_map/reduce_sum | solution.py:144
  304.3 6.1 %all-gather.5 = f32[2,3,2048]{2,1,0:T(4,128)S(1)} all-gather(f32[1,3,2048]{2,1,0:T(4,128)S(1)} %maximum_bitcast_fusion), channel_id=2, replica_groups=mesh['ctx_0'=2,'ctx_1'=4,'ctx_2'=2,'vocab_0'=2,'vocab_1'=4] {'ctx_0'}, dimensions={0}, use_global_device_ids=true | all-gather | bytes 73728 | tf_op jit(solution)/shard_map/all_gather | solution.py:42
  310.5 12.0 %all-gather.6 = f32[4,3,2048]{2,1,0:T(4,128)S(1)} all-gather(f32[1,3,2048]{2,1,0:T(4,128)S(1)} %maximum_bitcast_fusion.1), channel_id=3, replica_groups=mesh['ctx_0'=2,'ctx_1'=4,'ctx_2'=2,'vocab_0'=2,'vocab_1'=4] {'ctx_1'}, dimensions={0}, use_global_device_ids=true | all-gather | bytes 122880 | tf_op jit(solution)/shard_map/all_gather | solution.py:42
  322.7 1.9 all-gather.7
  324.6 4.6 %all-gather.8 = f32[2,3,2048]{2,1,0:T(4,128)S(1)} all-gather(f32[1,3,2048]{2,1,0:T(4,128)S(1)} %maximum_bitcast_fusion.3), channel_id=5, replica_groups=mesh['ctx_0'=2,'ctx_1'=4,'ctx_2'=2,'vocab_0'=2,'vocab_1'=4] {'vocab_0'}, dimensions={0}, use_global_device_ids=true | all-gather | bytes 73728 | tf_op jit(solution)/shard_map/all_gather | solution.py:42
  329.3 12.5 %all-gather.9 = f32[4,3,2048]{2,1,0:T(4,128)S(1)} all-gather(f32[1,3,2048]{2,1,0:T(4,128)S(1)} %maximum_bitcast_fusion.4), channel_id=6, replica_groups=mesh['ctx_0'=2,'ctx_1'=4,'ctx_2'=2,'vocab_0'=2,'vocab_1'=4] {'vocab_1'}, dimensions={0}, use_global_device_ids=true | all-gather | bytes 122880 | tf_op jit(solution)/shard_map/all_gather | solution.py:42
  341.9 0.6 dynamic-slice_subtract_fusion
  (59 shorter events, 3.1 us)
Async XLA Ops:
  7.2 72.3 %copy-start = (bf16[32,768]{1,0:T(8,128)(2,1)S(1)}, bf16[32,768]{1,0:T(8,128)(2,1)}, u32[]{:S(2)}) copy-start(bf16[32,768]{1,0:T(8,128)(2,1)} %param.11) | copy-start | bytes 147460
  7.2 80.4 %copy-start.2 = (bf16[16,6144]{1,0:T(8,128)(2,1)S(1)}, bf16[16,6144]{1,0:T(8,128)(2,1)}, u32[]{:S(2)}) copy-start(bf16[16,6144]{1,0:T(8,128)(2,1)} %param.16) | copy-start | bytes 589828
  7.2 80.5 %copy-start.3 = (bf16[16,6144]{1,0:T(8,128)(2,1)S(1)}, bf16[16,6144]{1,0:T(8,128)(2,1)}, u32[]{:S(2)}) copy-start(bf16[16,6144]{1,0:T(8,128)(2,1)} %param.15) | copy-start | bytes 589828
  7.2 80.5 %copy-start.4 = (bf16[16,6144]{1,0:T(8,128)(2,1)S(1)}, bf16[16,6144]{1,0:T(8,128)(2,1)}, u32[]{:S(2)}) copy-start(bf16[16,6144]{1,0:T(8,128)(2,1)} %param.17) | copy-start | bytes 589828
  9.0 71.0 %all-to-all-start = ((bf16[16,32,768]{2,1,0:T(8,128)(2,1)}), bf16[16,32,768]{2,1,0:T(8,128)(2,1)S(1)}, u32[]{:S(2)}, u32[]{:S(2)}) async-start(bf16[16,32,768]{2,1,0:T(8,128)(2,1)} %stack.2), calls=%async_computation | async-start | bytes 1572864 | tf_op jit(solution)/shard_map/all_to_all | solution.py:114
  79.2 16.2 %copy-start.1 = (bf16[16,6144]{1,0:T(8,128)(2,1)S(1)}, bf16[16,6144]{1,0:T(8,128)(2,1)}, u32[]{:S(2)}) copy-start(bf16[16,6144]{1,0:T(8,128)(2,1)} %param.18) | copy-start | bytes 589828
  79.5 16.2 %copy-start.5 = (f32[6144]{0:T(1024)S(1)}, f32[6144]{0:T(1024)}, u32[]{:S(2)}) copy-start(f32[6144]{0:T(1024)} %param.19) | copy-start | bytes 73732
  82.0 11.7 %all-to-all-start.1 = ((bf16[8,4,768]{2,1,0:T(4,128)(2,1)}), bf16[8,4,768]{2,1,0:T(4,128)(2,1)S(1)}, u32[]{:S(2)}, u32[]{:S(2)}) async-start(bf16[8,4,768]{2,1,0:T(4,128)(2,1)} %convert_element_type.30), calls=%async_computation.1 | async-start | bytes 98304 | tf_op jit(solution)/shard_map/all_to_all | solution.py:135
  87.4 178.1 %all-gather.12.cloned.1.call-start = ((), (), s32[]{:S(2)}) async-start(), calls=%async_computation.3 | async-start | bytes 26738688 | tf_op jit(solution)/shard_map/all_gather | solution.py:141
  87.7 32.1 %copy-start.6 = (s32[2048]{0:T(1024)S(1)}, s32[2048]{0:T(1024)}, u32[]{:S(2)}) copy-start(s32[2048]{0:T(1024)} %param.21) | copy-start | bytes 24580
Sparse Core Ops, SparseCore 0:
  120.0 145.5 all-gather.11
